TPU v7x, 32 devices: a whole 2x2x4 slice. The times are simulated.
32 devices in a mesh: parts: 2 (over y), clip: 4 (over x, core), tensor: 4 (over z).
Axes of the slice: x: 2, y: 2, z: 4, core: 2. Of those that a mesh axis runs over, the one named last changes fastest.
Arguments:
- clips: bfloat16 [32, 128, 4096], P(('parts', 'clip'), None, 'tensor'), parts along dimension 0, may hold values from -6 to 6
- targets: bfloat16 [32, 128, 4096], P(('parts', 'clip'), None, 'tensor'), parts along dimension 0, may hold values from -6 to 6
- lengths: int32 [32], P(('parts', 'clip')), parts along dimension 0, may hold values from 32 to 128, as said below
- gate_weight: bfloat16 [4096, 7168], P(None, 'tensor'), may hold values from -0.09375 to 0.09375
- up_weight: bfloat16 [4096, 7168], P(None, 'tensor'), may hold values from -0.09375 to 0.09375
- down_weight: bfloat16 [7168, 4096], P('tensor'), may hold values from -0.0625 to 0.0625
- proj_in: bfloat16 [64, 7168], P(None, 'tensor'), may hold values from -0.0625 to 0.0625
- proj_out: bfloat16 [64, 4096], replicated, may hold values from -0.09375 to 0.09375
- inv_hessian: bfloat16 [4096, 4096], P('clip', 'tensor'), may hold values from -0.2 to 2.2, as said below
- test_sketches: bfloat16 [4096, 4096], P('clip', 'tensor'), may hold values from -6 to 6
Outputs:
- scores: float32 [32, 4096], P(('parts', 'clip'), 'tensor'), parts along dimension 0
There are 2 independent parts, one for each index of `parts`. A program takes and returns all parts, laid end to end along the dimension named above; an argument that names none is the same for every part. Nothing has to cross between parts.
Inputs may be any that keep to these rules, and one draw needn't show every extreme that they name: `lengths`: every clip has between 32 and 128 valid tokens; in each part one clip has exactly 128 and another exactly 32. `inv_hessian`: the same matrix in both parts.
All inputs are finite; a program needn't handle non-finite values.
Results may differ from a plain program's by a relative error of at most 0.0066.
Values may be sent and summed in bfloat16 or wider, within the bound.
A program may use at most 192 MiB of HBM per device.

v0:
```python
import jax
import jax.numpy as jnp
from jax import lax
from jax.sharding import PartitionSpec as P


def on_device(
    clips,
    targets,
    lengths,
    gate_weight,
    up_weight,
    down_weight,
    proj_in,
    proj_out,
    inv_hessian,
    test_sketches,
):
    clip_count, slot_count, width_part = clips.shape
    row_count = clip_count * slot_count
    proj_size = proj_in.shape[0]
    flat_tokens = clips.reshape(row_count, width_part)
    piece = lax.all_gather(flat_tokens, "tensor", axis=1, tiled=True)
    gate_act = jnp.dot(piece, gate_weight, preferred_element_type=jnp.float32)
    up_act = jnp.dot(piece, up_weight, preferred_element_type=jnp.float32)
    hidden = (jax.nn.silu(gate_act) * up_act).astype(jnp.bfloat16)
    left_part = jnp.dot(hidden, proj_in.T, preferred_element_type=jnp.float32)
    tensor_pos = lax.axis_index("tensor")
    lens_float = lengths.astype(jnp.float32)
    partial_out = jnp.dot(hidden, down_weight, preferred_element_type=jnp.float32)
    outputs = lax.psum_scatter(partial_out, "tensor", scatter_dimension=1, tiled=True)
    position = jnp.arange(slot_count, dtype=jnp.int32)
    masked = (position[None, :] < lengths[:, None]).astype(jnp.float32) / lens_float[:, None]
    golden = targets.reshape(row_count, width_part).astype(jnp.float32)
    differ = jnp.clip(outputs - golden, -1.0, 1.0)
    grad_out = (differ * masked.reshape(row_count)[:, None]).astype(jnp.bfloat16)
    proj_cols = lax.dynamic_slice_in_dim(proj_out, tensor_pos * width_part, width_part, 1)
    right_part = jnp.dot(grad_out, proj_cols.T, preferred_element_type=jnp.float32)
    joined = lax.psum(jnp.concatenate([left_part, right_part], axis=1), "tensor")
    left_full = joined[:, :proj_size].reshape(clip_count, slot_count, proj_size)
    right_full = joined[:, proj_size:].reshape(clip_count, slot_count, proj_size)
    sketch = jnp.einsum("cti,ctk->cik", left_full, right_full, precision=lax.Precision.HIGHEST)
    flat_sketch = sketch.reshape(clip_count, proj_size * proj_size).astype(jnp.bfloat16)
    precond = jnp.dot(
        flat_sketch,
        lax.all_gather(inv_hessian, "clip", axis=0, tiled=True),
        preferred_element_type=jnp.float32,
    ).astype(jnp.bfloat16)
    partial_scores = lax.dot_general(
        precond,
        lax.all_gather(test_sketches, "clip", axis=0, tiled=True),
        (((1,), (1,)), ((), ())),
        preferred_element_type=jnp.float32,
    )
    return lax.psum_scatter(partial_scores, "tensor", scatter_dimension=1, tiled=True)


def solution(mesh):
    in_specs = (
        P(("parts", "clip"), None, "tensor"),
        P(("parts", "clip"), None, "tensor"),
        P(("parts", "clip")),
        P(None, "tensor"),
        P(None, "tensor"),
        P("tensor", None),
        P(None, "tensor"),
        P(),
        P("clip", "tensor"),
        P("clip", "tensor"),
    )
    out_specs = P(("parts", "clip"), "tensor")
    return jax.shard_map(
        on_device, mesh=mesh, in_specs=in_specs, out_specs=out_specs, check_vma=False
    )
```

profile of v0, /device:TPU:0, one launch (start us, length us, event | category | flops | bytes accessed | tf_op | source)
XLA Modules:
  0.0 461.4 jit_solution(14233535387168297329)
XLA Ops:
  7.4 0.0 copy-start
  7.4 0.0 all-gather.4.cloned.1.call-start
  7.4 0.7 all-gather.4.cloned.1.call-update
  8.1 0.0 reduce-scatter.5.cloned.1.call-start
  8.1 85.1 %all-gather.4.cloned.1.call-done = bf16[512,4096]{1,0:T(8,128)(2,1)} async-done(((bf16[512,1024]{1,0:T(8,128)(2,1)}), bf16[512,4096]{1,0:T(8,128)(2,1)}) %all-gather.4.cloned.1.call-update) | async-done | bytes 4194320 | tf_op jit(solution)/shard_map/all_gather | solution.py:23
  93.3 0.0 copy-start.3
  93.3 0.0 slice-start
  93.3 0.0 slice-start.1
  93.3 14.7 %fusion.10 = f32[512,1792]{1,0:T(8,128)} fusion(bf16[512,4096]{1,0:T(8,128)(2,1)} %all-gather.4.cloned.1.call-done, bf16[4096,1792]{1,0:T(8,128)(2,1)} %param.13), kind=kOutput, calls=%fused_computation.20 | convolution fusion | flops 7516192768 | bytes 22544384 | tf_op jit(solution)/shard_map/dot_general | solution.py:24
  107.9 0.0 copy-done.3
  107.9 0.0 slice-start.2
  107.9 0.0 slice-start.3
  107.9 12.8 %multiply_convert_fusion = bf16[512,1792]{1,0:T(8,128)(2,1)S(1)} fusion(f32[512,1792]{1,0:T(8,128)} %fusion.10, bf16[512,4096]{1,0:T(8,128)(2,1)S(1)} %copy-done.3, bf16[4096,1792]{1,0:T(8,128)(2,1)} %param.14), kind=kOutput, calls=%fused_computation.1 | convolution fusion | flops 7521697792 | bytes 24379392 | tf_op jit(solution)/shard_map/dot_general | solution.py:25
  120.8 0.0 slice-done
  120.8 0.0 slice-done.1
  120.8 0.0 slice-done.2
  120.8 0.0 slice-done.3
  120.8 9.9 %fusion.12 = f32[512,4096]{1,0:T(8,128)} fusion(bf16[512,1792]{1,0:T(8,128)(2,1)S(1)} %multiply_convert_fusion, bf16[1792,4096]{1,0:T(8,128)(2,1)S(1)} %bitcast.34), kind=kOutput, calls=%fused_computation.22 | convolution fusion | flops 7516192768 | bytes 24903680 | tf_op jit(solution)/shard_map/dot_general | solution.py:30
  130.8 0.0 copy-start.2
  130.8 0.0 copy-start.1
  130.8 0.0 reduce-scatter.5.cloned.1.call-update
  130.8 0.0 all-reduce.2.cloned.1.call-start
  130.9 0.6 copy-done.2
  131.4 0.1 divide_bitcast_fusion
  131.5 1.6 fusion.11
  133.1 140.9 %reduce-scatter.5.cloned.1.call-done = f32[512,1024]{1,0:T(8,128)} async-done(((f32[512,4096]{1,0:T(8,128)}), f32[512,1024]{1,0:T(8,128)}) %reduce-scatter.5.cloned.1.call-update) | async-done | bytes 2097168 | tf_op jit(solution)/shard_map/reduce_scatter | solution.py:31
  274.0 0.0 copy-done.1
  274.0 1.9 fusion.2
  275.9 0.0 copy-done
  275.9 0.4 fusion.7
  276.4 0.7 pad_maximum_fusion
  277.1 0.0 all-reduce.2.cloned.1.call-update
  277.1 0.0 all-gather.6.cloned.1.call-start
  277.2 0.5 all-gather.6.cloned.1.call-update
  277.7 0.0 all-gather.8.cloned.1.call-start
  277.7 0.5 all-gather.8.cloned.1.call-update
  278.3 0.2 reduce-scatter.7.cloned.1.call-start
  278.5 34.8 %all-reduce.2.cloned.1.call-done = f32[512,128]{0,1:T(8,128)} async-done(((f32[512,128]{0,1:T(8,128)}), f32[512,128]{0,1:T(8,128)}) %all-reduce.2.cloned.1.call-update) | async-done | bytes 262160 | tf_op jit(solution)/shard_map/psum | solution.py:39
  313.3 1.0 slice_bitcast_fusion.1
  314.3 0.3 convolution_convert_fusion
  314.6 0.1 convert_element_type.39
  314.7 23.4 %all-gather.6.cloned.1.call-done = bf16[4096,1024]{1,0:T(8,128)(2,1)} async-done(((bf16[1024,1024]{1,0:T(8,128)(2,1)}), bf16[4096,1024]{1,0:T(8,128)(2,1)}) %all-gather.6.cloned.1.call-update) | async-done | bytes 8388624 | tf_op jit(solution)/shard_map/all_gather | solution.py:46
  338.1 59.7 %all-gather.8.cloned.1.call-done = bf16[4096,1024]{1,0:T(8,128)(2,1)} async-done(((bf16[1024,1024]{1,0:T(8,128)(2,1)}), bf16[4096,1024]{1,0:T(8,128)(2,1)}) %all-gather.8.cloned.1.call-update) | async-done | bytes 8388624 | tf_op jit(solution)/shard_map/all_gather | solution.py:51
  397.8 10.6 %convolution_bitcast_fusion = f32[4096,4]{1,0:T(8,128)} fusion(bf16[4096,1024]{1,0:T(8,128)(2,1)} %all-gather.8.cloned.1.call-done, bf16[4,4096]{1,0:T(4,128)(2,1)S(1)} %convert_element_type.39, bf16[4096,1024]{1,0:T(8,128)(2,1)} %all-gather.6.cloned.1.call-done), kind=kOutput, calls=%fused_computation | convolution fusion | flops 67112960 | bytes 16875520
  408.4 0.0 reduce-scatter.7.cloned.1.call-update
  408.4 44.0 %reduce-scatter.7.cloned.1.call-done = f32[1024,4]{1,0:T(8,128)} async-done(((f32[4096,4]{1,0:T(8,128)}), f32[1024,4]{1,0:T(8,128)}) %reduce-scatter.7.cloned.1.call-update) | async-done | bytes 16400
  452.4 1.8 copy.16
  (2 shorter events, 0.0 us)
Async XLA Ops:
  7.4 268.5 %copy-start = (bf16[64,4096]{1,0:T(8,128)(2,1)S(1)}, bf16[64,4096]{1,0:T(8,128)(2,1)}, u32[]{:S(2)}) copy-start(bf16[64,4096]{1,0:T(8,128)(2,1)} %param.17) | copy-start | bytes 1572868
  7.4 85.9 %all-gather.4.cloned.1.call-start = ((), (), s32[]{:S(2)}) async-start(), calls=%async_computation.2 | async-start | bytes 5242880 | tf_op jit(solution)/shard_map/all_gather | solution.py:23
  8.1 265.9 %reduce-scatter.5.cloned.1.call-start = ((), (), s32[]{:S(2)}) async-start(), calls=%async_computation.3 | async-start | bytes 10485760 | tf_op jit(solution)/shard_map/reduce_scatter | solution.py:31
  93.3 14.7 %copy-start.3 = (bf16[512,4096]{1,0:T(8,128)(2,1)S(1)}, bf16[512,4096]{1,0:T(8,128)(2,1)}, u32[]{:S(2)}) copy-start(bf16[512,4096]{1,0:T(8,128)(2,1)} %all-gather.4.cloned.1.call-done) | copy-start | bytes 12582916
  93.3 27.5 %slice-start = ((s8[14680064]{0:T(1024)(128)(4,1)}), s8[4194304]{0:T(1024)(128)(4,1)S(1)}, s32[]{:S(2)}) async-start(s8[14680064]{0:T(1024)(128)(4,1)} %bitcast.33), calls=%async_computation.8 | async-start | bytes 8388608
  93.3 27.5 %slice-start.1 = ((s8[14680064]{0:T(1024)(128)(4,1)}), s8[4194304]{0:T(1024)(128)(4,1)S(1)}, s32[]{:S(2)}) async-start(s8[14680064]{0:T(1024)(128)(4,1)} %bitcast.33), calls=%async_computation.9 | async-start | bytes 8388608
  107.9 12.9 %slice-start.2 = ((s8[14680064]{0:T(1024)(128)(4,1)}), s8[4194304]{0:T(1024)(128)(4,1)S(1)}, s32[]{:S(2)}) async-start(s8[14680064]{0:T(1024)(128)(4,1)} %bitcast.33), calls=%async_computation.10 | async-start | bytes 8388608
  107.9 12.9 %slice-start.3 = ((s8[14680064]{0:T(1024)(128)(4,1)}), s8[2097152]{0:T(1024)(128)(4,1)S(1)}, s32[]{:S(2)}) async-start(s8[14680064]{0:T(1024)(128)(4,1)} %bitcast.33), calls=%async_computation.11 | async-start | bytes 4194304
  130.8 0.7 copy-start.2
  130.8 143.2 %copy-start.1 = (bf16[4,128,1024]{2,1,0:T(8,128)(2,1)S(1)}, bf16[4,128,1024]{2,1,0:T(8,128)(2,1)}, u32[]{:S(2)}) copy-start(bf16[4,128,1024]{2,1,0:T(8,128)(2,1)} %param.11) | copy-start | bytes 3145732
  130.8 182.5 %all-reduce.2.cloned.1.call-start = ((), (), s32[]{:S(2)}) async-start(), calls=%async_computation.4 | async-start | bytes 524288 | tf_op jit(solution)/shard_map/psum | solution.py:39
  277.1 61.0 %all-gather.6.cloned.1.call-start = ((), (), s32[]{:S(2)}) async-start(), calls=%async_computation.5 | async-start | bytes 10485760 | tf_op jit(solution)/shard_map/all_gather | solution.py:46
  277.7 120.1 %all-gather.8.cloned.1.call-start = ((), (), s32[]{:S(2)}) async-start(), calls=%async_computation.6 | async-start | bytes 10485760 | tf_op jit(solution)/shard_map/all_gather | solution.py:51
  278.3 174.1 %reduce-scatter.7.cloned.1.call-start = ((), (), s32[]{:S(2)}) async-start(), calls=%async_computation.7 | async-start | bytes 2621440
Sparse Core Ops, SparseCore 0:
  9.8 83.4 all-gather.3
  130.9 143.0 reduce-scatter.4
  277.2 36.0 all-reduce.1
  408.5 43.8 reduce-scatter.6
Sparse Core Ops, SparseCore 1:
  279.2 58.8 all-gather.5
  339.6 58.1 all-gather.7
where the time goes:
time: 462 us; the launch traced here: 461 us
  waiting for transfers between devices  390 us (84%)
  matrix products  50.4 us (11%)
  between operations  14.7 us (3%)
    reduce_scatter x1, waiting for transfers between devices, on_device(): lax.psum_scatter(partial_out, 'tensor', scatter_dimension=1, tiled=True)  141 us
    all_gather x1, waiting for transfers between devices, on_device(): piece = lax.all_gather(flat_tokens, 'tensor', axis=1, tiled=True)  85.1 us
    all_gather x1, waiting for transfers between devices, on_device(): lax.all_gather(test_sketches, 'clip', axis=0, tiled=True)  59.7 us
    unnamed x7, waiting for transfers between devices  45.8 us
    psum x1, waiting for transfers between devices, on_device(): lax.psum(jnp.concatenate([left_part, right_part], axis=1), 'tensor')  34.8 us
    all_gather x1, waiting for transfers between devices, on_device(): lax.all_gather(inv_hessian, 'clip', axis=0, tiled=True)  23.4 us
    dot_general x1, matrix products, on_device(): gate_act = jnp.dot(piece, gate_weight, preferred_element_type=jnp.float32)  14.7 us
    dot_general x1, matrix products, on_device(): up_act = jnp.dot(piece, up_weight, preferred_element_type=jnp.float32)  12.8 us
  transfers between devices with their start and end apart: 6, of which 6 were waited for; matrix products, arithmetic and copies ran while one was open for 1% of the time, Pallas kernels for 0%

commit v1 on v0

--- a/solution.py
+++ b/solution.py
@@ -2,6 +2,19 @@
 import jax.numpy as jnp
 from jax import lax
 from jax.sharding import PartitionSpec as P
+
+
+def gather_around(array, axis, dim):
+    ways = lax.axis_size(axis)
+    up = [(d, (d + 1) % ways) for d in range(ways)]
+    down = [(d, (d - 1) % ways) for d in range(ways)]
+    earlier, later = ([array], [array])
+    for _ in range(ways // 2):
+        earlier.append(lax.ppermute(earlier[-1], axis, up))
+    for _ in range((ways - 1) // 2):
+        later.append(lax.ppermute(later[-1], axis, down))
+    line = jnp.concatenate([*earlier[::-1], *later[1:]], axis=dim)
+    return jnp.roll(line, (lax.axis_index(axis) - ways // 2) * array.shape[dim], axis=dim)
 
 
 def on_device(
@@ -42,9 +55,7 @@
     sketch = jnp.einsum("cti,ctk->cik", left_full, right_full, precision=lax.Precision.HIGHEST)
     flat_sketch = sketch.reshape(clip_count, proj_size * proj_size).astype(jnp.bfloat16)
     precond = jnp.dot(
-        flat_sketch,
-        lax.all_gather(inv_hessian, "clip", axis=0, tiled=True),
-        preferred_element_type=jnp.float32,
+        flat_sketch, gather_around(inv_hessian, "clip", 0), preferred_element_type=jnp.float32
     ).astype(jnp.bfloat16)
     partial_scores = lax.dot_general(
         precond,

time: 462 us -> 481 us (1.041)
  local copies, waits for them, and re-layouts: 3.53 us -> 25.4 us
    ppermute x0 -> x3, waiting for transfers between devices: none -> 112 us  [the longest x2 112 us: gather_around(): earlier.append(lax.ppermute(earlier[-1], axis, up))]
    all_gather x1, waiting for transfers between devices: 59.7 us -> 0.03 us  [on_device(): lax.all_gather(test_sketches, 'clip', axis=0, tiled=True)]
    psum x1, waiting for transfers between devices: 34.8 us -> 0.01 us  [on_device(): lax.psum(jnp.concatenate([left_part, right_part], axis=1), 'tensor')]
    all_gather x1 -> x0, waiting for transfers between devices: 23.4 us -> none  [on_device(): lax.all_gather(inv_hessian, 'clip', axis=0, tiled=True)]
    unnamed x18 -> x27, local copies, waits for them, and re-layouts: 3.42 us -> 22.2 us
    unnamed x7 -> x6, waiting for transfers between devices: 45.8 us -> 47.3 us
  transfers between devices with their start and end apart: 6 -> 8, of which waited for: 6 -> 5; matrix products, arithmetic and copies ran while one was open for 1% -> 5% of each run, Pallas kernels for 0% -> 0%
where the time goes in v1:
time: 481 us
  waiting for transfers between devices  386 us (80%)
  matrix products  49.6 us (10%)
  local copies, waits for them, and re-layouts  25.4 us (5%)
  between operations  14.7 us (3%)
    reduce_scatter x1, waiting for transfers between devices, on_device(): lax.psum_scatter(partial_out, 'tensor', scatter_dimension=1, tiled=True)  142 us
    ppermute x2, waiting for transfers between devices, gather_around(): earlier.append(lax.ppermute(earlier[-1], axis, up))  112 us
    all_gather x1, waiting for transfers between devices, on_device(): piece = lax.all_gather(flat_tokens, 'tensor', axis=1, tiled=True)  85.1 us
    unnamed x6, waiting for transfers between devices  47.3 us
    unnamed x27, local copies, waits for them, and re-layouts  22.2 us
    dot_general x1, matrix products, on_device(): gate_act = jnp.dot(piece, gate_weight, preferred_element_type=jnp.float32)  14.7 us
    dot_general x1, matrix products, on_device(): up_act = jnp.dot(piece, up_weight, preferred_element_type=jnp.float32)  12.8 us
    unnamed x1, matrix products  10.7 us
  transfers between devices with their start and end apart: 8, of which 5 were waited for; matrix products, arithmetic and copies ran while one was open for 5% of the time, Pallas kernels for 0%

profile of v1, /device:TPU:0, one launch (start us, length us, event | category | flops | bytes accessed | tf_op | source)
XLA Modules:
  0.0 481.0 jit_solution(9944647733755991728)
XLA Ops:
  7.4 0.0 copy-start
  7.4 0.0 all-gather.3.cloned.1.call-start
  7.4 0.7 all-gather.3.cloned.1.call-update
  8.1 0.0 reduce-scatter.5.cloned.1.call-start
  8.1 85.1 %all-gather.3.cloned.1.call-done = bf16[512,4096]{1,0:T(8,128)(2,1)} async-done(((bf16[512,1024]{1,0:T(8,128)(2,1)}), bf16[512,4096]{1,0:T(8,128)(2,1)}) %all-gather.3.cloned.1.call-update) | async-done | bytes 4194320 | tf_op jit(solution)/shard_map/all_gather | solution.py:36
  93.3 14.7 %fusion.19 = f32[512,1792]{1,0:T(8,128)} fusion(bf16[512,4096]{1,0:T(8,128)(2,1)} %all-gather.3.cloned.1.call-done, bf16[4096,1792]{1,0:T(8,128)(2,1)} %param.13), kind=kOutput, calls=%fused_computation.31 | convolution fusion | flops 7516192768 | bytes 22544384 | tf_op jit(solution)/shard_map/dot_general | solution.py:37
  108.0 0.0 copy-done.4
  108.0 12.8 %multiply_convert_fusion = bf16[512,1792]{1,0:T(8,128)(2,1)S(1)} fusion(f32[512,1792]{1,0:T(8,128)} %fusion.19, bf16[512,4096]{1,0:T(8,128)(2,1)S(1)} %copy-done.4, bf16[4096,1792]{1,0:T(8,128)(2,1)} %param.14), kind=kOutput, calls=%fused_computation.3 | convolution fusion | flops 7521697792 | bytes 24379392 | tf_op jit(solution)/shard_map/dot_general | solution.py:38
  120.8 0.0 slice-done
  120.8 0.0 slice-done.1
  120.8 10.0 %fusion.21 = f32[512,4096]{1,0:T(8,128)} fusion(bf16[512,1792]{1,0:T(8,128)(2,1)S(1)} %multiply_convert_fusion, bf16[1792,4096]{1,0:T(8,128)(2,1)S(1)} %bitcast.33), kind=kOutput, calls=%fused_computation.33 | convolution fusion | flops 7516192768 | bytes 24903680 | tf_op jit(solution)/shard_map/dot_general | solution.py:43
  130.8 0.0 reduce-scatter.5.cloned.1.call-update
  130.8 0.0 all-reduce.2.cloned.1.call-start
  130.9 0.6 copy-done.3
  131.5 0.1 divide_bitcast_fusion
  131.5 0.2 copy-done.2
  131.8 0.7 fusion.20
  132.4 0.0 copy-start.1
  132.4 141.5 %reduce-scatter.5.cloned.1.call-done = f32[512,1024]{1,0:T(8,128)} async-done(((f32[512,4096]{1,0:T(8,128)}), f32[512,1024]{1,0:T(8,128)}) %reduce-scatter.5.cloned.1.call-update) | async-done | bytes 2097168 | tf_op jit(solution)/shard_map/reduce_scatter | solution.py:44
  274.0 2.2 fusion.4
  276.2 0.4 fusion.14
  276.6 0.7 pad_maximum_fusion
  277.3 0.0 all-reduce.2.cloned.1.call-update
  277.4 0.0 all-gather.5.cloned.1.call-start
  277.4 0.5 all-gather.5.cloned.1.call-update
  277.9 0.0 reduce-scatter.7.cloned.1.call-start
  278.0 0.1 collective-permute-start
  278.1 49.0 %collective-permute-done = bf16[1024,1024]{1,0:T(8,128)(2,1)} collective-permute-done((bf16[1024,1024]{1,0:T(8,128)(2,1)S(1)}, bf16[1024,1024]{1,0:T(8,128)(2,1)}, u32[]{:S(2)}, u32[]{:S(2)}) %collective-permute-start) | collective-permute-done | bytes 2097184 | tf_op jit(solution)/shard_map/ppermute | solution.py:13
  327.1 1.3 collective-permute-start.1
  328.4 0.4 collective-permute-start.2
  328.9 63.4 %collective-permute-done.1 = bf16[1024,1024]{1,0:T(8,128)(2,1)} collective-permute-done((bf16[1024,1024]{1,0:T(8,128)(2,1)}, bf16[1024,1024]{1,0:T(8,128)(2,1)}, u32[]{:S(2)}, u32[]{:S(2)}) %collective-permute-start.1) | collective-permute-done | bytes 2097184 | tf_op jit(solution)/shard_map/ppermute | solution.py:13
  392.2 3.1 constant_dynamic-update-slice_fusion.7
  395.3 3.1 constant_dynamic-update-slice_fusion.6
  398.4 1.5 constant_dynamic-update-slice_fusion.5
  399.9 0.0 collective-permute-done.2
  399.9 3.1 constant_dynamic-update-slice_fusion.4
  403.0 3.2 constant_dynamic-update-slice_fusion.3
  406.2 3.1 constant_dynamic-update-slice_fusion.2
  409.3 1.5 constant_dynamic-update-slice_fusion.1
  410.8 3.1 constant_dynamic-update-slice_fusion
  413.8 1.0 slice_bitcast_fusion.1
  414.8 0.3 convolution_convert_fusion
  415.2 0.1 convert_element_type.39
  415.3 0.0 all-gather.5.cloned.1.call-done
  415.3 10.7 %convolution_bitcast_fusion = f32[4096,4]{1,0:T(8,128)} fusion(bf16[4096,1024]{1,0:T(8,128)(2,1)} %all-gather.5.cloned.1.call-done, bf16[4,4096]{1,0:T(4,128)(2,1)S(1)} %convert_element_type.39, bf16[8192,1024]{1,0:T(8,128)(2,1)} %constant_dynamic-update-slice_fusion, s32[]{:T(128)S(6)} %select_n.18), kind=kOutput, calls=%fused_computation.2 | convolution fusion | flops 67112960 | bytes 16875524
  426.0 0.0 reduce-scatter.7.cloned.1.call-update
  426.0 46.0 %reduce-scatter.7.cloned.1.call-done = f32[1024,4]{1,0:T(8,128)} async-done(((f32[4096,4]{1,0:T(8,128)}), f32[1024,4]{1,0:T(8,128)}) %reduce-scatter.7.cloned.1.call-update) | async-done | bytes 16400
  472.1 1.8 copy.16
  (14 shorter events, 0.0 us)
Async XLA Ops:
  7.4 268.8 %copy-start = (bf16[64,4096]{1,0:T(8,128)(2,1)S(1)}, bf16[64,4096]{1,0:T(8,128)(2,1)}, u32[]{:S(2)}) copy-start(bf16[64,4096]{1,0:T(8,128)(2,1)} %param.17) | copy-start | bytes 1572868
  7.4 85.9 %all-gather.3.cloned.1.call-start = ((), (), s32[]{:S(2)}) async-start(), calls=%async_computation.2 | async-start | bytes 5242880 | tf_op jit(solution)/shard_map/all_gather | solution.py:36
  8.1 265.9 %reduce-scatter.5.cloned.1.call-start = ((), (), s32[]{:S(2)}) async-start(), calls=%async_computation.3 | async-start | bytes 10485760 | tf_op jit(solution)/shard_map/reduce_scatter | solution.py:44
  93.3 14.7 %copy-start.4 = (bf16[512,4096]{1,0:T(8,128)(2,1)S(1)}, bf16[512,4096]{1,0:T(8,128)(2,1)}, u32[]{:S(2)}) copy-start(bf16[512,4096]{1,0:T(8,128)(2,1)} %all-gather.3.cloned.1.call-done) | copy-start | bytes 12582916
  93.3 27.5 %slice-start = ((s8[14680064]{0:T(1024)(128)(4,1)}), s8[4194304]{0:T(1024)(128)(4,1)S(1)}, s32[]{:S(2)}) async-start(s8[14680064]{0:T(1024)(128)(4,1)} %bitcast.32), calls=%async_computation.7 | async-start | bytes 8388608
  93.3 27.5 %slice-start.1 = ((s8[14680064]{0:T(1024)(128)(4,1)}), s8[4194304]{0:T(1024)(128)(4,1)S(1)}, s32[]{:S(2)}) async-start(s8[14680064]{0:T(1024)(128)(4,1)} %bitcast.32), calls=%async_computation.8 | async-start | bytes 8388608
  108.0 12.9 %slice-start.2 = ((s8[14680064]{0:T(1024)(128)(4,1)}), s8[4194304]{0:T(1024)(128)(4,1)S(1)}, s32[]{:S(2)}) async-start(s8[14680064]{0:T(1024)(128)(4,1)} %bitcast.32), calls=%async_computation.9 | async-start | bytes 8388608
  108.0 12.9 %slice-start.3 = ((s8[14680064]{0:T(1024)(128)(4,1)}), s8[2097152]{0:T(1024)(128)(4,1)S(1)}, s32[]{:S(2)}) async-start(s8[14680064]{0:T(1024)(128)(4,1)} %bitcast.32), calls=%async_computation.10 | async-start | bytes 4194304
  130.8 0.7 copy-start.3
  130.8 1.0 copy-start.2
  130.8 283.0 %all-reduce.2.cloned.1.call-start = ((), (), s32[]{:S(2)}) async-start(), calls=%async_computation.4 | async-start | bytes 524288 | tf_op jit(solution)/shard_map/psum | solution.py:52
  132.4 145.6 %copy-start.1 = (bf16[1024,1024]{1,0:T(8,128)(2,1)S(1)}, bf16[1024,1024]{1,0:T(8,128)(2,1)}, u32[]{:S(2)}) copy-start(bf16[1024,1024]{1,0:T(8,128)(2,1)} %param.18) | copy-start | bytes 6291460
  277.4 138.0 %all-gather.5.cloned.1.call-start = ((), (), s32[]{:S(2)}) async-start(), calls=%async_computation.5 | async-start | bytes 10485760 | tf_op jit(solution)/shard_map/all_gather | solution.py:62
  277.9 194.1 %reduce-scatter.7.cloned.1.call-start = ((), (), s32[]{:S(2)}) async-start(), calls=%async_computation.6 | async-start | bytes 2621440
  278.0 49.1 %collective-permute-start = (bf16[1024,1024]{1,0:T(8,128)(2,1)S(1)}, bf16[1024,1024]{1,0:T(8,128)(2,1)}, u32[]{:S(2)}, u32[]{:S(2)}) collective-permute-start(bf16[1024,1024]{1,0:T(8,128)(2,1)S(1)} %copy-done.1), channel_id=1, source_target_pairs={{0,4},{4,8},{8,12},{12,0},{1,5},{5,9},{9,13},{13,1},{2,6},{6,10},{... | collective-permute-start | bytes 6291464 | tf_op jit(solution)/shard_map/ppermute | solution.py:13
  327.1 65.1 %collective-permute-start.1 = (bf16[1024,1024]{1,0:T(8,128)(2,1)}, bf16[1024,1024]{1,0:T(8,128)(2,1)}, u32[]{:S(2)}, u32[]{:S(2)}) collective-permute-start(bf16[1024,1024]{1,0:T(8,128)(2,1)} %collective-permute-done), channel_id=1, source_target_pairs={{0,4},{4,8},{8,12},{12,0},{1,5},{5,9},{9,13},{13,1},{2,6},{6,10},{... | collective-permute-start | bytes 6291464 | tf_op jit(solution)/shard_map/ppermute | solution.py:13
  328.4 71.4 %collective-permute-start.2 = (bf16[1024,1024]{1,0:T(8,128)(2,1)S(1)}, bf16[1024,1024]{1,0:T(8,128)(2,1)}, u32[]{:S(2)}, u32[]{:S(2)}) collective-permute-start(bf16[1024,1024]{1,0:T(8,128)(2,1)S(1)} %copy-done.1), channel_id=1, source_target_pairs={{0,12},{4,0},{8,4},{12,8},{1,13},{5,1},{9,5},{13,9},{2,14},{6,2},{... | collective-permute-start | bytes 6291464 | tf_op jit(solution)/shard_map/ppermute | solution.py:15
Sparse Core Ops, SparseCore 0:
  9.8 83.4 all-gather.2
  131.0 142.9 reduce-scatter.4
  277.5 36.0 all-reduce.1
  426.1 45.8 reduce-scatter.6
Sparse Core Ops, SparseCore 1:
  279.5 87.6 all-gather.4
